TPU v7x, 32 devices: a whole 2x2x4 slice. The times are simulated.
32 devices in a mesh: row: 8 (over y, x, core), rep: 4 (over z).
Axes of the slice: x: 2, y: 2, z: 4, core: 2. Of those that a mesh axis runs over, the one named last changes fastest.
Arguments:
- features: float32 [16384, 256], P('row'), may hold values from -6 to 6
- adjacency_tiles: float32 [8, 4, 256, 128, 128], P('row', 'rep'), may hold values from -0.25 to 0.25
- tile_rows: int32 [8, 4, 256], P('row', 'rep'), may hold values from 0 to 15, as said below
- tile_cols: int32 [8, 4, 256], P('row', 'rep'), may hold values from 0 to 31, as said below
- tile_counts: int32 [8, 4], P('row', 'rep'), may hold values from 32 to 256, as said below
- plan: int32 [4, 2], replicated, may hold values from 0 to 7, as said below
- weights: float32 [2, 256, 256], replicated, may hold values from -0.375 to 0.375
Outputs:
- embedded: float32 [16384, 256], P(('row', 'rep'))
Inputs may be any that keep to these rules, and one draw needn't show every extreme that they name: Within one block row and replica the listed positions (tile_rows, tile_cols) are distinct. Within one block row and replica the listed positions (tile_rows, tile_cols) are distinct. `tile_counts`: some block row and replica lists exactly 256 tiles. `plan`: every block row 0 to 7 appears exactly once in the table.
All inputs are finite; a program needn't handle non-finite values.
Results may differ from a plain program's by a relative error of at most 0.0003.
Values sent between devices are 32-bit elements; how exact they have to be, the bound alone decides.
No kernel may reach another device: no remote copies, remote signals or barrier semaphores. Data moves between devices by JAX's collectives and lax.ppermute only.
A program may use at most 128 MiB of HBM per device.

v0:
```python
import math
import jax
import jax.numpy as jnp
from jax import lax
from jax.sharding import PartitionSpec as P


def from_root(value, axis, source):
    kept = jnp.where(lax.axis_index(axis) == source, value, 0).astype(value.dtype)
    return lax.psum(kept, axis)


def tile_sum(received, tiles_here, rows_here, cols_here, count_here, row_tiles):
    tile_slots = tiles_here.shape[0]
    tile_edge = received.shape[1]
    feat_width = received.shape[2]
    group_size = math.gcd(tile_slots, 64)
    steps_total = tile_slots // group_size
    slot_ids = jnp.arange(tile_slots, dtype=jnp.int32)
    live_mask = (slot_ids < count_here).astype(jnp.float32)
    lane_ids = jnp.arange(row_tiles, dtype=jnp.int32)

    def advance(running, packet):
        block_tiles, block_rows, block_cols, block_live = packet
        sources = jnp.take(received, block_cols, axis=0)
        product = jnp.einsum("tij,tjf->tif", block_tiles, sources, precision=lax.Precision.HIGHEST)
        product = product * block_live[:, None, None]
        placing = (block_rows[None, :] == lane_ids[:, None]).astype(jnp.float32)
        added = jnp.dot(
            placing,
            product.reshape(group_size, tile_edge * feat_width),
            precision=lax.Precision.HIGHEST,
        )
        return (running + added, None)

    packets = (
        tiles_here.reshape(steps_total, group_size, tile_edge, tile_edge),
        rows_here.reshape(steps_total, group_size),
        cols_here.reshape(steps_total, group_size),
        live_mask.reshape(steps_total, group_size),
    )
    start = jnp.zeros((row_tiles, tile_edge * feat_width), jnp.float32)
    running, unused = lax.scan(advance, start, packets)
    return running.reshape(row_tiles * tile_edge, feat_width)


def shards(features, adjacency_tiles, tile_rows, tile_cols, tile_counts, plan, weights):
    replica = lax.axis_index("rep")
    block_len = features.shape[0]
    feat_width = features.shape[1]
    tile_edge = adjacency_tiles.shape[-1]
    row_tiles = block_len // tile_edge
    section_total = plan.shape[1]
    layer_total = weights.shape[0]
    section_roots = lax.dynamic_index_in_dim(plan, replica, 0, keepdims=False)
    tiles_here = adjacency_tiles[0, 0]
    rows_here = tile_rows[0, 0]
    cols_here = tile_cols[0, 0]
    count_here = tile_counts[0, 0]
    current = features
    result = features
    for layer_num in range(layer_total):
        received = jnp.zeros((section_total * block_len, feat_width), jnp.float32)
        for section_num in range(section_total):
            root_now = lax.dynamic_index_in_dim(section_roots, section_num, 0, keepdims=False)
            arrived = from_root(current, "row", root_now)
            received = lax.dynamic_update_slice_in_dim(
                received, arrived, section_num * block_len, 0
            )
        received = received.reshape(section_total * row_tiles, tile_edge, feat_width)
        partial_value = tile_sum(received, tiles_here, rows_here, cols_here, count_here, row_tiles)
        my_share = lax.psum_scatter(partial_value, "rep", scatter_dimension=0, tiled=True)
        result = jnp.maximum(
            jnp.dot(my_share, weights[layer_num], precision=lax.Precision.HIGHEST), 0.0
        )
        if layer_num + 1 < layer_total:
            current = lax.all_gather(result, "rep", axis=0, tiled=True)
    return result


def solution(mesh):
    return jax.shard_map(
        shards,
        mesh=mesh,
        in_specs=(
            P("row", None),
            P("row", "rep", None, None, None),
            P("row", "rep", None),
            P("row", "rep", None),
            P("row", "rep"),
            P(),
            P(),
        ),
        out_specs=P(("row", "rep"), None),
        check_vma=False,
    )
```

profile of v0, /device:TPU:0, one launch (start us, length us, event | category | flops | bytes accessed | tf_op | source)
XLA Modules:
  0.0 589.2 jit_solution(12762534406502106215)
XLA Ops:
  6.5 0.7 copy-done
  9.0 3.9 broadcast_select_fusion.3
  15.7 81.0 %all-reduce.7.cloned.1.call-done = (f32[2048,256]{1,0:T(8,128)}, f32[2048,256]{1,0:T(8,128)}) async-done(((f32[2048,256]{1,0:T(8,128)}, f32[2048,256]{1,0:T(8,128)}), (f32[2048,256]{1,0:T(8,128)}, f32[2048,256]{1,0:T(8,128)})) %all-reduce.7.cloned.1.call-update) | async-done | bytes 4194320 | tf_op jit(solution)/shard_map/psum | solution.py:10
  96.6 4.5 pad_maximum_fusion
  101.1 126.4 %while.22 = (s32[]{:T(128)}, f32[16,32768]{1,0:T(8,128)S(1)}, s32[4,64]{1,0:T(4,128)S(1)}, f32[4,64,128,128]{3,2,1,0:T(8,128)}, s32[4,64]{1,0:T(4,128)S(1)}, /*i...) while((s32[]{:T(128)}, f32[16,32768]{1,0:T(8,128)S(1)}, ...), condition=%wide.region_3.5_spmd.clone, body=%wide.region_2.4_spmd.clone.sunk | while | flops 3629124096 | bytes 67116272 | solution.py:43
  101.1 6.5 %gather_fusion = f32[64,128,256]{2,1,0:T(8,128)} fusion(f32[32,128,256]{2,1,0:T(8,128)} %get-tuple-element.303, s32[1024]{0:T(1024)S(1)} %pad_clamp_fusion.4), kind=kCustom, calls=%fused_computation.clone.clone.1 | custom fusion | bytes 16777472 | tf_op jit(solution)/shard_map/while/body/eval_jaxpr/jit(_take)/gather | solution.py:25
  107.6 11.7 %broadcast_multiply_fusion.4 = f32[64,128,256]{2,1,0:T(8,128)S(1)} fusion(f32[64]{0:T(128)S(1)} %fusion.59, f32[64,128,256]{2,1,0:T(8,128)} %gather_fusion, pred[64]{0:T(512)(128)(4,1)S(1)} %get-tuple-element.270, f32[4,64,128,128]{3,2,1,0:T(8,128)} %get-tuple-element.301, s32[]{:T(128)} %get-tuple-element.289), kind=kOutput, calls=%fused_computation.9.clone.1 | convolution fusion | flops 3225419776 | bytes 20972352 | tf_op jit(solution)/shard_map/while/body/eval_jaxpr/tij,tjf->tif/dot_general | solution.py:26
  119.4 8.0 %copy.12 = f32[8,8,128,256]{3,1,2,0:T(8,128)} copy(f32[8,8,128,256]{3,2,1,0:T(8,128)S(1)} %bitcast.75) | data formatting | bytes 16777216 | tf_op jit(solution)/shard_map/while
  127.3 5.3 convolution_add_fusion.4
  132.7 6.5 %gather_fusion = f32[64,128,256]{2,1,0:T(8,128)} fusion(f32[32,128,256]{2,1,0:T(8,128)} %get-tuple-element.303, s32[1024]{0:T(1024)S(1)} %pad_clamp_fusion.4), kind=kCustom, calls=%fused_computation.clone.clone.1 | custom fusion | bytes 16777472 | tf_op jit(solution)/shard_map/while/body/eval_jaxpr/jit(_take)/gather | solution.py:25
  139.2 11.7 %broadcast_multiply_fusion.4 = f32[64,128,256]{2,1,0:T(8,128)S(1)} fusion(f32[64]{0:T(128)S(1)} %fusion.59, f32[64,128,256]{2,1,0:T(8,128)} %gather_fusion, pred[64]{0:T(512)(128)(4,1)S(1)} %get-tuple-element.270, f32[4,64,128,128]{3,2,1,0:T(8,128)} %get-tuple-element.301, s32[]{:T(128)} %get-tuple-element.289), kind=kOutput, calls=%fused_computation.9.clone.1 | convolution fusion | flops 3225419776 | bytes 20972352 | tf_op jit(solution)/shard_map/while/body/eval_jaxpr/tij,tjf->tif/dot_general | solution.py:26
  151.0 8.0 %copy.12 = f32[8,8,128,256]{3,1,2,0:T(8,128)} copy(f32[8,8,128,256]{3,2,1,0:T(8,128)S(1)} %bitcast.75) | data formatting | bytes 16777216 | tf_op jit(solution)/shard_map/while
  158.9 5.3 convolution_add_fusion.4
  164.3 6.5 %gather_fusion = f32[64,128,256]{2,1,0:T(8,128)} fusion(f32[32,128,256]{2,1,0:T(8,128)} %get-tuple-element.303, s32[1024]{0:T(1024)S(1)} %pad_clamp_fusion.4), kind=kCustom, calls=%fused_computation.clone.clone.1 | custom fusion | bytes 16777472 | tf_op jit(solution)/shard_map/while/body/eval_jaxpr/jit(_take)/gather | solution.py:25
  170.8 11.7 %broadcast_multiply_fusion.4 = f32[64,128,256]{2,1,0:T(8,128)S(1)} fusion(f32[64]{0:T(128)S(1)} %fusion.59, f32[64,128,256]{2,1,0:T(8,128)} %gather_fusion, pred[64]{0:T(512)(128)(4,1)S(1)} %get-tuple-element.270, f32[4,64,128,128]{3,2,1,0:T(8,128)} %get-tuple-element.301, s32[]{:T(128)} %get-tuple-element.289), kind=kOutput, calls=%fused_computation.9.clone.1 | convolution fusion | flops 3225419776 | bytes 20972352 | tf_op jit(solution)/shard_map/while/body/eval_jaxpr/tij,tjf->tif/dot_general | solution.py:26
  182.6 8.0 %copy.12 = f32[8,8,128,256]{3,1,2,0:T(8,128)} copy(f32[8,8,128,256]{3,2,1,0:T(8,128)S(1)} %bitcast.75) | data formatting | bytes 16777216 | tf_op jit(solution)/shard_map/while
  190.6 5.3 convolution_add_fusion.4
  196.0 6.5 %gather_fusion = f32[64,128,256]{2,1,0:T(8,128)} fusion(f32[32,128,256]{2,1,0:T(8,128)} %get-tuple-element.303, s32[1024]{0:T(1024)S(1)} %pad_clamp_fusion.4), kind=kCustom, calls=%fused_computation.clone.clone.1 | custom fusion | bytes 16777472 | tf_op jit(solution)/shard_map/while/body/eval_jaxpr/jit(_take)/gather | solution.py:25
  202.5 11.7 %broadcast_multiply_fusion.4 = f32[64,128,256]{2,1,0:T(8,128)S(1)} fusion(f32[64]{0:T(128)S(1)} %fusion.59, f32[64,128,256]{2,1,0:T(8,128)} %gather_fusion, pred[64]{0:T(512)(128)(4,1)S(1)} %get-tuple-element.270, f32[4,64,128,128]{3,2,1,0:T(8,128)} %get-tuple-element.301, s32[]{:T(128)} %get-tuple-element.289), kind=kOutput, calls=%fused_computation.9.clone.1 | convolution fusion | flops 3225419776 | bytes 20972352 | tf_op jit(solution)/shard_map/while/body/eval_jaxpr/tij,tjf->tif/dot_general | solution.py:26
  214.2 8.0 %copy.12 = f32[8,8,128,256]{3,1,2,0:T(8,128)} copy(f32[8,8,128,256]{3,2,1,0:T(8,128)S(1)} %bitcast.75) | data formatting | bytes 16777216 | tf_op jit(solution)/shard_map/while
  222.2 5.3 convolution_add_fusion.4
  227.5 1.5 reshape.37
  229.3 43.6 %reduce-scatter.3.cloned.1.call-done = f32[512,256]{1,0:T(8,128)} async-done(((f32[2048,256]{1,0:T(8,128)}), f32[512,256]{1,0:T(8,128)}) %reduce-scatter.3.cloned.1.call-update) | async-done | bytes 524304 | tf_op jit(solution)/shard_map/reduce_scatter | solution.py:72
  272.9 2.4 convolution_maximum_fusion.1
  275.4 45.0 %all-gather.2.cloned.1.call-done = f32[2048,256]{1,0:T(8,128)} async-done(((f32[512,256]{1,0:T(8,128)}), f32[2048,256]{1,0:T(8,128)}) %all-gather.2.cloned.1.call-update) | async-done | bytes 2097168 | tf_op jit(solution)/shard_map/all_gather | solution.py:77
  320.4 3.8 broadcast_select_fusion.1
  324.3 79.7 %all-reduce.5.cloned.1.call-done = (f32[2048,256]{1,0:T(8,128)}, f32[2048,256]{1,0:T(8,128)}) async-done(((f32[2048,256]{1,0:T(8,128)}, f32[2048,256]{1,0:T(8,128)}), (f32[2048,256]{1,0:T(8,128)}, f32[2048,256]{1,0:T(8,128)})) %all-reduce.5.cloned.1.call-update) | async-done | bytes 4194320 | tf_op jit(solution)/shard_map/psum | solution.py:10
  404.0 4.5 pad_maximum_fusion.1
  408.5 126.4 %while.23 = (s32[]{:T(128)}, f32[16,32768]{1,0:T(8,128)S(1)}, s32[4,64]{1,0:T(4,128)S(1)}, f32[4,64,128,128]{3,2,1,0:T(8,128)}, s32[4,64]{1,0:T(4,128)S(1)}, /*i...) while((s32[]{:T(128)}, f32[16,32768]{1,0:T(8,128)S(1)}, ...), condition=%wide.region_8.10_spmd.clone, body=%wide.region_7.9_spmd.clone.sunk | while | flops 3629124096 | bytes 67116272 | solution.py:43
  408.5 6.5 %gather_fusion.1 = f32[64,128,256]{2,1,0:T(8,128)} fusion(f32[32,128,256]{2,1,0:T(8,128)} %get-tuple-element.330, s32[1024]{0:T(1024)S(1)} %pad_clamp_fusion.5), kind=kCustom, calls=%fused_computation.1.clone.clone.1 | custom fusion | bytes 16777472 | tf_op jit(solution)/shard_map/while/body/eval_jaxpr/jit(_take)/gather | solution.py:25
  415.0 11.7 %broadcast_multiply_fusion.5 = f32[64,128,256]{2,1,0:T(8,128)S(1)} fusion(f32[64]{0:T(128)S(1)} %fusion.64, f32[64,128,256]{2,1,0:T(8,128)} %gather_fusion.1, pred[64]{0:T(512)(128)(4,1)S(1)} %get-tuple-element.279, f32[4,64,128,128]{3,2,1,0:T(8,128)} %get-tuple-element.328, s32[]{:T(128)} %get-tuple-element.316), kind=kOutput, calls=%fused_computation.30.clone.1 | convolution fusion | flops 3225419776 | bytes 20972352 | tf_op jit(solution)/shard_map/while/body/eval_jaxpr/tij,tjf->tif/dot_general | solution.py:26
  426.8 8.0 %copy.13 = f32[8,8,128,256]{3,1,2,0:T(8,128)} copy(f32[8,8,128,256]{3,2,1,0:T(8,128)S(1)} %bitcast.76) | data formatting | bytes 16777216 | tf_op jit(solution)/shard_map/while
  434.7 5.3 convolution_add_fusion.5
  440.1 6.5 %gather_fusion.1 = f32[64,128,256]{2,1,0:T(8,128)} fusion(f32[32,128,256]{2,1,0:T(8,128)} %get-tuple-element.330, s32[1024]{0:T(1024)S(1)} %pad_clamp_fusion.5), kind=kCustom, calls=%fused_computation.1.clone.clone.1 | custom fusion | bytes 16777472 | tf_op jit(solution)/shard_map/while/body/eval_jaxpr/jit(_take)/gather | solution.py:25
  446.6 11.7 %broadcast_multiply_fusion.5 = f32[64,128,256]{2,1,0:T(8,128)S(1)} fusion(f32[64]{0:T(128)S(1)} %fusion.64, f32[64,128,256]{2,1,0:T(8,128)} %gather_fusion.1, pred[64]{0:T(512)(128)(4,1)S(1)} %get-tuple-element.279, f32[4,64,128,128]{3,2,1,0:T(8,128)} %get-tuple-element.328, s32[]{:T(128)} %get-tuple-element.316), kind=kOutput, calls=%fused_computation.30.clone.1 | convolution fusion | flops 3225419776 | bytes 20972352 | tf_op jit(solution)/shard_map/while/body/eval_jaxpr/tij,tjf->tif/dot_general | solution.py:26
  458.4 8.0 %copy.13 = f32[8,8,128,256]{3,1,2,0:T(8,128)} copy(f32[8,8,128,256]{3,2,1,0:T(8,128)S(1)} %bitcast.76) | data formatting | bytes 16777216 | tf_op jit(solution)/shard_map/while
  466.3 5.3 convolution_add_fusion.5
  471.7 6.5 %gather_fusion.1 = f32[64,128,256]{2,1,0:T(8,128)} fusion(f32[32,128,256]{2,1,0:T(8,128)} %get-tuple-element.330, s32[1024]{0:T(1024)S(1)} %pad_clamp_fusion.5), kind=kCustom, calls=%fused_computation.1.clone.clone.1 | custom fusion | bytes 16777472 | tf_op jit(solution)/shard_map/while/body/eval_jaxpr/jit(_take)/gather | solution.py:25
  478.2 11.7 %broadcast_multiply_fusion.5 = f32[64,128,256]{2,1,0:T(8,128)S(1)} fusion(f32[64]{0:T(128)S(1)} %fusion.64, f32[64,128,256]{2,1,0:T(8,128)} %gather_fusion.1, pred[64]{0:T(512)(128)(4,1)S(1)} %get-tuple-element.279, f32[4,64,128,128]{3,2,1,0:T(8,128)} %get-tuple-element.328, s32[]{:T(128)} %get-tuple-element.316), kind=kOutput, calls=%fused_computation.30.clone.1 | convolution fusion | flops 3225419776 | bytes 20972352 | tf_op jit(solution)/shard_map/while/body/eval_jaxpr/tij,tjf->tif/dot_general | solution.py:26
  490.0 8.0 %copy.13 = f32[8,8,128,256]{3,1,2,0:T(8,128)} copy(f32[8,8,128,256]{3,2,1,0:T(8,128)S(1)} %bitcast.76) | data formatting | bytes 16777216 | tf_op jit(solution)/shard_map/while
  497.9 5.3 convolution_add_fusion.5
  503.3 6.5 %gather_fusion.1 = f32[64,128,256]{2,1,0:T(8,128)} fusion(f32[32,128,256]{2,1,0:T(8,128)} %get-tuple-element.330, s32[1024]{0:T(1024)S(1)} %pad_clamp_fusion.5), kind=kCustom, calls=%fused_computation.1.clone.clone.1 | custom fusion | bytes 16777472 | tf_op jit(solution)/shard_map/while/body/eval_jaxpr/jit(_take)/gather | solution.py:25
  509.8 11.7 %broadcast_multiply_fusion.5 = f32[64,128,256]{2,1,0:T(8,128)S(1)} fusion(f32[64]{0:T(128)S(1)} %fusion.64, f32[64,128,256]{2,1,0:T(8,128)} %gather_fusion.1, pred[64]{0:T(512)(128)(4,1)S(1)} %get-tuple-element.279, f32[4,64,128,128]{3,2,1,0:T(8,128)} %get-tuple-element.328, s32[]{:T(128)} %get-tuple-element.316), kind=kOutput, calls=%fused_computation.30.clone.1 | convolution fusion | flops 3225419776 | bytes 20972352 | tf_op jit(solution)/shard_map/while/body/eval_jaxpr/tij,tjf->tif/dot_general | solution.py:26
  521.6 8.0 %copy.13 = f32[8,8,128,256]{3,1,2,0:T(8,128)} copy(f32[8,8,128,256]{3,2,1,0:T(8,128)S(1)} %bitcast.76) | data formatting | bytes 16777216 | tf_op jit(solution)/shard_map/while
  529.6 5.3 convolution_add_fusion.5
  534.9 1.5 reshape.39
  536.4 43.8 %reduce-scatter.5.cloned.1.call-done = f32[512,256]{1,0:T(8,128)} async-done(((f32[2048,256]{1,0:T(8,128)}), f32[512,256]{1,0:T(8,128)}) %reduce-scatter.5.cloned.1.call-update) | async-done | bytes 524304 | tf_op jit(solution)/shard_map/reduce_scatter | solution.py:72
  580.3 2.4 convolution_maximum_fusion
  (61 shorter events, 3.3 us)
Async XLA Ops:
  6.5 0.7 copy-start
  6.5 90.1 %all-reduce.7.cloned.1.call-start = ((), (), s32[]{:S(2)}) async-start(), calls=%async_computation.6 | async-start | bytes 8388608 | tf_op jit(solution)/shard_map/psum | solution.py:10
  9.0 4.5 copy-start.3
  9.0 5.2 copy-start.4
  12.9 260.0 %reduce-scatter.3.cloned.1.call-start = ((), (), s32[]{:S(2)}) async-start(), calls=%async_computation.2 | async-start | bytes 2621440 | tf_op jit(solution)/shard_map/reduce_scatter | solution.py:72
  227.5 45.4 %copy-start.2 = (f32[2,256,256]{2,1,0:T(8,128)S(1)}, f32[2,256,256]{2,1,0:T(8,128)}, u32[]{:S(2)}) copy-start(f32[2,256,256]{2,1,0:T(8,128)} %param.19) | copy-start | bytes 1572868
  229.1 91.3 %all-gather.2.cloned.1.call-start = ((), (), s32[]{:S(2)}) async-start(), calls=%async_computation.3 | async-start | bytes 2621440 | tf_op jit(solution)/shard_map/all_gather | solution.py:77
  275.4 128.7 %all-reduce.5.cloned.1.call-start = ((), (), s32[]{:S(2)}) async-start(), calls=%async_computation.5 | async-start | bytes 8388608 | tf_op jit(solution)/shard_map/psum | solution.py:10
  324.2 256.1 %reduce-scatter.5.cloned.1.call-start = ((), (), s32[]{:S(2)}) async-start(), calls=%async_computation.4 | async-start | bytes 2621440 | tf_op jit(solution)/shard_map/reduce_scatter | solution.py:72
  534.9 47.8 %copy-start.1 = (s32[4,2]{0,1:T(2,128)S(1)}, s32[4,2]{0,1:T(2,128)}, u32[]{:S(2)}) copy-start(s32[4,2]{0,1:T(2,128)} %param.18) | copy-start | bytes 100
Sparse Core Ops, SparseCore 0:
  13.0 83.5 all-reduce.6
  229.2 43.6 reduce-scatter.2
  275.5 44.8 all-gather.1
  324.4 79.6 all-reduce.4
  536.6 43.6 reduce-scatter.4
where the time goes:
time: 590 us; the launch traced here: 589 us
  waiting for transfers between devices  293 us (50%)
  matrix products  141 us (24%)
  local copies, waits for them, and re-layouts  121 us (21%)
  other arithmetic  18.1 us (3%)
  between operations  15.1 us (3%)
    psum x2, waiting for transfers between devices, from_root(): return lax.psum(kept, axis)  161 us
    dot_general x8, matrix products, advance(): jnp.einsum('tij,tjf->tif', block_tiles, sources, precision=lax.Precision....  93.9 us
    reduce_scatter x2, waiting for transfers between devices, shards(): lax.psum_scatter(partial_value, 'rep', scatter_dimension=0, tiled=True)  87.5 us
    while x8, local copies, waits for them, and re-layouts  63.7 us
    gather x8, local copies, waits for them, and re-layouts, advance(): sources = jnp.take(received, block_cols, axis=0)  52 us
    all_gather x1, waiting for transfers between devices, shards(): current = lax.all_gather(result, 'rep', axis=0, tiled=True)  45 us
    dot_general x8, matrix products, advance(): jnp.dot(placing, product.reshape(group_size, tile_edge * feat_width), pre...  42.7 us
  transfers between devices with their start and end apart: 5, of which 5 were waited for; matrix products, arithmetic and copies ran while one was open for 0% of the time, Pallas kernels for 0%

commit v1 on v0

--- a/solution.py
+++ b/solution.py
@@ -7,7 +7,7 @@
 
 def from_root(value, axis, source):
     kept = jnp.where(lax.axis_index(axis) == source, value, 0).astype(value.dtype)
-    return lax.psum(kept, axis)
+    return jnp.sum(lax.all_gather(kept, axis), axis=0)
 
 
 def tile_sum(received, tiles_here, rows_here, cols_here, count_here, row_tiles):

time: 590 us -> 808 us (1.37)
  waiting for transfers between devices: 293 us -> 477 us
  other arithmetic: 18.1 us -> 52.2 us
    all_gather x0 -> x4, waiting for transfers between devices: none -> 343 us  [from_root(): return jnp.sum(lax.all_gather(kept, axis), axis=0)]
    psum x2 -> x0, waiting for transfers between devices: 161 us -> none  [from_root(): return lax.psum(kept, axis)]
    reduce_sum x0 -> x4, other arithmetic: none -> 34 us  [from_root(): return jnp.sum(lax.all_gather(kept, axis), axis=0)]
  transfers between devices with their start and end apart: 5 -> 7, of which waited for: 5 -> 7; matrix products, arithmetic and copies ran while one was open for 0% -> 2% of each run, Pallas kernels for 0% -> 0%
where the time goes in v1:
time: 808 us
  waiting for transfers between devices  477 us (59%)
  matrix products  141 us (17%)
  local copies, waits for them, and re-layouts  121 us (15%)
  other arithmetic  52.2 us (6%)
  between operations  15.5 us (2%)
    all_gather x4, waiting for transfers between devices, from_root(): return jnp.sum(lax.all_gather(kept, axis), axis=0)  343 us
    dot_general x8, matrix products, advance(): jnp.einsum('tij,tjf->tif', block_tiles, sources, precision=lax.Precision....  93.9 us
    reduce_scatter x2, waiting for transfers between devices, shards(): lax.psum_scatter(partial_value, 'rep', scatter_dimension=0, tiled=True)  87.3 us
    while x8, local copies, waits for them, and re-layouts  63.7 us
    gather x8, local copies, waits for them, and re-layouts, advance(): sources = jnp.take(received, block_cols, axis=0)  52 us
    all_gather x1, waiting for transfers between devices, shards(): current = lax.all_gather(result, 'rep', axis=0, tiled=True)  45 us
    dot_general x8, matrix products, advance(): jnp.dot(placing, product.reshape(group_size, tile_edge * feat_width), pre...  42.7 us
    reduce_sum x4, other arithmetic, from_root(): return jnp.sum(lax.all_gather(kept, axis), axis=0)  34 us
  transfers between devices with their start and end apart: 7, of which 7 were waited for; matrix products, arithmetic and copies ran while one was open for 2% of the time, Pallas kernels for 0%

profile of v1, /device:TPU:0, one launch (start us, length us, event | category | flops | bytes accessed | tf_op | source)
XLA Modules:
  0.0 807.7 jit_solution(13728828844367373214)
XLA Ops:
  9.2 3.9 broadcast_select_fusion.3
  16.6 89.1 %all-gather.12.cloned.1.call-done = f32[16384,256]{1,0:T(8,128)} async-done(((f32[2048,256]{1,0:T(8,128)}), f32[16384,256]{1,0:T(8,128)}) %all-gather.12.cloned.1.call-update) | async-done | bytes 16777232 | tf_op jit(solution)/shard_map/all_gather | solution.py:10
  105.7 8.5 %reduce_sum.36 = f32[2048,256]{1,0:T(8,128)} reduce(f32[8,2048,256]{2,1,0:T(8,128)} %bitcast.84, f32[]{:T(128)} %constant.65.clone.1), dimensions={0}, to_apply=%region_0.1 | reduce | flops 3670016 | bytes 18874372 | tf_op jit(solution)/shard_map/reduce_sum | solution.py:10
  114.3 83.1 %all-gather.14.cloned.1.call-done = f32[16384,256]{1,0:T(8,128)} async-done(((f32[2048,256]{1,0:T(8,128)}), f32[16384,256]{1,0:T(8,128)}) %all-gather.14.cloned.1.call-update) | async-done | bytes 16777232 | tf_op jit(solution)/shard_map/all_gather | solution.py:10
  197.4 8.5 %reduce_sum.37 = f32[2048,256]{1,0:T(8,128)} reduce(f32[8,2048,256]{2,1,0:T(8,128)} %bitcast.85, f32[]{:T(128)} %constant.65.clone.1), dimensions={0}, to_apply=%region_1.2 | reduce | flops 3670016 | bytes 18874372 | tf_op jit(solution)/shard_map/reduce_sum | solution.py:10
  205.8 4.5 pad_maximum_fusion
  210.3 126.4 %while.22 = (s32[]{:T(128)}, f32[16,32768]{1,0:T(8,128)S(1)}, s32[4,64]{1,0:T(4,128)S(1)}, f32[4,64,128,128]{3,2,1,0:T(8,128)}, s32[4,64]{1,0:T(4,128)S(1)}, /*i...) while((s32[]{:T(128)}, f32[16,32768]{1,0:T(8,128)S(1)}, ...), condition=%wide.region_3.5_spmd.clone, body=%wide.region_2.4_spmd.clone.sunk | while | flops 3629124096 | bytes 67116272 | solution.py:43
  210.3 6.5 gather_fusion
  216.8 11.7 %broadcast_multiply_fusion.4 = f32[64,128,256]{2,1,0:T(8,128)S(1)} fusion(f32[64]{0:T(128)S(1)} %fusion.59, f32[64,128,256]{2,1,0:T(8,128)} %gather_fusion, pred[64]{0:T(512)(128)(4,1)S(1)} %get-tuple-element.266, f32[4,64,128,128]{3,2,1,0:T(8,128)} %get-tuple-element.297, s32[]{:T(128)} %get-tuple-element.285), kind=kOutput, calls=%fused_computation.9.clone.1 | convolution fusion | flops 3225419776 | bytes 20972352 | tf_op jit(solution)/shard_map/while/body/eval_jaxpr/tij,tjf->tif/dot_general | solution.py:26
  228.6 8.0 copy.12
  236.6 5.3 convolution_add_fusion.4
  242.0 6.5 gather_fusion
  248.5 11.7 %broadcast_multiply_fusion.4 = f32[64,128,256]{2,1,0:T(8,128)S(1)} fusion(f32[64]{0:T(128)S(1)} %fusion.59, f32[64,128,256]{2,1,0:T(8,128)} %gather_fusion, pred[64]{0:T(512)(128)(4,1)S(1)} %get-tuple-element.266, f32[4,64,128,128]{3,2,1,0:T(8,128)} %get-tuple-element.297, s32[]{:T(128)} %get-tuple-element.285), kind=kOutput, calls=%fused_computation.9.clone.1 | convolution fusion | flops 3225419776 | bytes 20972352 | tf_op jit(solution)/shard_map/while/body/eval_jaxpr/tij,tjf->tif/dot_general | solution.py:26
  260.2 8.0 copy.12
  268.2 5.3 convolution_add_fusion.4
  273.6 6.5 gather_fusion
  280.1 11.7 %broadcast_multiply_fusion.4 = f32[64,128,256]{2,1,0:T(8,128)S(1)} fusion(f32[64]{0:T(128)S(1)} %fusion.59, f32[64,128,256]{2,1,0:T(8,128)} %gather_fusion, pred[64]{0:T(512)(128)(4,1)S(1)} %get-tuple-element.266, f32[4,64,128,128]{3,2,1,0:T(8,128)} %get-tuple-element.297, s32[]{:T(128)} %get-tuple-element.285), kind=kOutput, calls=%fused_computation.9.clone.1 | convolution fusion | flops 3225419776 | bytes 20972352 | tf_op jit(solution)/shard_map/while/body/eval_jaxpr/tij,tjf->tif/dot_general | solution.py:26
  291.8 8.0 copy.12
  299.8 5.3 convolution_add_fusion.4
  305.2 6.5 gather_fusion
  311.7 11.7 %broadcast_multiply_fusion.4 = f32[64,128,256]{2,1,0:T(8,128)S(1)} fusion(f32[64]{0:T(128)S(1)} %fusion.59, f32[64,128,256]{2,1,0:T(8,128)} %gather_fusion, pred[64]{0:T(512)(128)(4,1)S(1)} %get-tuple-element.266, f32[4,64,128,128]{3,2,1,0:T(8,128)} %get-tuple-element.297, s32[]{:T(128)} %get-tuple-element.285), kind=kOutput, calls=%fused_computation.9.clone.1 | convolution fusion | flops 3225419776 | bytes 20972352 | tf_op jit(solution)/shard_map/while/body/eval_jaxpr/tij,tjf->tif/dot_general | solution.py:26
  323.4 8.0 copy.12
  331.4 5.3 convolution_add_fusion.4
  338.6 43.5 %reduce-scatter.3.cloned.1.call-done = f32[512,256]{1,0:T(8,128)} async-done(((f32[2048,256]{1,0:T(8,128)}), f32[512,256]{1,0:T(8,128)}) %reduce-scatter.3.cloned.1.call-update) | async-done | bytes 524304 | tf_op jit(solution)/shard_map/reduce_scatter | solution.py:72
  384.6 45.0 %all-gather.10.cloned.1.call-done = f32[2048,256]{1,0:T(8,128)} async-done(((f32[512,256]{1,0:T(8,128)}), f32[2048,256]{1,0:T(8,128)}) %all-gather.10.cloned.1.call-update) | async-done | bytes 2097168 | tf_op jit(solution)/shard_map/all_gather | solution.py:77
  434.1 88.1 %all-gather.16.cloned.1.call-done = f32[16384,256]{1,0:T(8,128)} async-done(((f32[2048,256]{1,0:T(8,128)}), f32[16384,256]{1,0:T(8,128)}) %all-gather.16.cloned.1.call-update) | async-done | bytes 16777232 | tf_op jit(solution)/shard_map/all_gather | solution.py:10
  522.2 8.5 %reduce_sum.38 = f32[2048,256]{1,0:T(8,128)} reduce(f32[8,2048,256]{2,1,0:T(8,128)} %bitcast.86, f32[]{:T(128)} %constant.65.clone.1), dimensions={0}, to_apply=%region_5.7 | reduce | flops 3670016 | bytes 18874372 | tf_op jit(solution)/shard_map/reduce_sum | solution.py:10
  530.7 83.0 %all-gather.18.cloned.1.call-done = f32[16384,256]{1,0:T(8,128)} async-done(((f32[2048,256]{1,0:T(8,128)}), f32[16384,256]{1,0:T(8,128)}) %all-gather.18.cloned.1.call-update) | async-done | bytes 16777232 | tf_op jit(solution)/shard_map/all_gather | solution.py:10
  613.7 8.5 %reduce_sum.39 = f32[2048,256]{1,0:T(8,128)} reduce(f32[8,2048,256]{2,1,0:T(8,128)} %bitcast.87, f32[]{:T(128)} %constant.65.clone.1), dimensions={0}, to_apply=%region_6.8 | reduce | flops 3670016 | bytes 18874372 | tf_op jit(solution)/shard_map/reduce_sum | solution.py:10
  622.2 4.5 pad_maximum_fusion.1
  626.6 126.4 %while.23 = (s32[]{:T(128)}, f32[16,32768]{1,0:T(8,128)S(1)}, s32[4,64]{1,0:T(4,128)S(1)}, f32[4,64,128,128]{3,2,1,0:T(8,128)}, s32[4,64]{1,0:T(4,128)S(1)}, /*i...) while((s32[]{:T(128)}, f32[16,32768]{1,0:T(8,128)S(1)}, ...), condition=%wide.region_8.10_spmd.clone, body=%wide.region_7.9_spmd.clone.sunk | while | flops 3629124096 | bytes 67116272 | solution.py:43
  626.7 6.5 gather_fusion.1
  633.2 11.7 %broadcast_multiply_fusion.5 = f32[64,128,256]{2,1,0:T(8,128)S(1)} fusion(f32[64]{0:T(128)S(1)} %fusion.64, f32[64,128,256]{2,1,0:T(8,128)} %gather_fusion.1, pred[64]{0:T(512)(128)(4,1)S(1)} %get-tuple-element.275, f32[4,64,128,128]{3,2,1,0:T(8,128)} %get-tuple-element.324, s32[]{:T(128)} %get-tuple-element.312), kind=kOutput, calls=%fused_computation.30.clone.1 | convolution fusion | flops 3225419776 | bytes 20972352 | tf_op jit(solution)/shard_map/while/body/eval_jaxpr/tij,tjf->tif/dot_general | solution.py:26
  644.9 8.0 copy.13
  652.9 5.3 convolution_add_fusion.5
  658.3 6.5 gather_fusion.1
  664.8 11.7 %broadcast_multiply_fusion.5 = f32[64,128,256]{2,1,0:T(8,128)S(1)} fusion(f32[64]{0:T(128)S(1)} %fusion.64, f32[64,128,256]{2,1,0:T(8,128)} %gather_fusion.1, pred[64]{0:T(512)(128)(4,1)S(1)} %get-tuple-element.275, f32[4,64,128,128]{3,2,1,0:T(8,128)} %get-tuple-element.324, s32[]{:T(128)} %get-tuple-element.312), kind=kOutput, calls=%fused_computation.30.clone.1 | convolution fusion | flops 3225419776 | bytes 20972352 | tf_op jit(solution)/shard_map/while/body/eval_jaxpr/tij,tjf->tif/dot_general | solution.py:26
  676.5 8.0 copy.13
  684.5 5.3 convolution_add_fusion.5
  689.9 6.5 gather_fusion.1
  696.4 11.7 %broadcast_multiply_fusion.5 = f32[64,128,256]{2,1,0:T(8,128)S(1)} fusion(f32[64]{0:T(128)S(1)} %fusion.64, f32[64,128,256]{2,1,0:T(8,128)} %gather_fusion.1, pred[64]{0:T(512)(128)(4,1)S(1)} %get-tuple-element.275, f32[4,64,128,128]{3,2,1,0:T(8,128)} %get-tuple-element.324, s32[]{:T(128)} %get-tuple-element.312), kind=kOutput, calls=%fused_computation.30.clone.1 | convolution fusion | flops 3225419776 | bytes 20972352 | tf_op jit(solution)/shard_map/while/body/eval_jaxpr/tij,tjf->tif/dot_general | solution.py:26
  708.1 8.0 copy.13
  716.1 5.3 convolution_add_fusion.5
  721.5 6.5 gather_fusion.1
  728.0 11.7 %broadcast_multiply_fusion.5 = f32[64,128,256]{2,1,0:T(8,128)S(1)} fusion(f32[64]{0:T(128)S(1)} %fusion.64, f32[64,128,256]{2,1,0:T(8,128)} %gather_fusion.1, pred[64]{0:T(512)(128)(4,1)S(1)} %get-tuple-element.275, f32[4,64,128,128]{3,2,1,0:T(8,128)} %get-tuple-element.324, s32[]{:T(128)} %get-tuple-element.312), kind=kOutput, calls=%fused_computation.30.clone.1 | convolution fusion | flops 3225419776 | bytes 20972352 | tf_op jit(solution)/shard_map/while/body/eval_jaxpr/tij,tjf->tif/dot_general | solution.py:26
  739.8 8.0 copy.13
  747.7 5.3 convolution_add_fusion.5
  754.6 43.8 %reduce-scatter.5.cloned.1.call-done = f32[512,256]{1,0:T(8,128)} async-done(((f32[2048,256]{1,0:T(8,128)}), f32[512,256]{1,0:T(8,128)}) %reduce-scatter.5.cloned.1.call-update) | async-done | bytes 524304 | tf_op jit(solution)/shard_map/reduce_scatter | solution.py:72
  (71 shorter events, 17.2 us)
Async XLA Ops:
  6.5 0.7 copy-start
  6.5 99.2 %all-gather.12.cloned.1.call-start = ((), (), s32[]{:S(2)}) async-start(), calls=%async_computation.5 | async-start | bytes 18874368 | tf_op jit(solution)/shard_map/all_gather | solution.py:10
  9.1 5.4 copy-start.3
  9.1 6.1 copy-start.4
  13.1 184.2 %all-gather.14.cloned.1.call-start = ((), (), s32[]{:S(2)}) async-start(), calls=%async_computation.6 | async-start | bytes 18874368 | tf_op jit(solution)/shard_map/all_gather | solution.py:10
  13.9 368.2 %reduce-scatter.3.cloned.1.call-start = ((), (), s32[]{:S(2)}) async-start(), calls=%async_computation.2 | async-start | bytes 2621440 | tf_op jit(solution)/shard_map/reduce_scatter | solution.py:72
  336.8 45.3 %copy-start.2 = (f32[2,256,256]{2,1,0:T(8,128)S(1)}, f32[2,256,256]{2,1,0:T(8,128)}, u32[]{:S(2)}) copy-start(f32[2,256,256]{2,1,0:T(8,128)} %param.19) | copy-start | bytes 1572868
  338.3 91.2 %all-gather.10.cloned.1.call-start = ((), (), s32[]{:S(2)}) async-start(), calls=%async_computation.3 | async-start | bytes 2621440 | tf_op jit(solution)/shard_map/all_gather | solution.py:77
  384.5 137.7 %all-gather.16.cloned.1.call-start = ((), (), s32[]{:S(2)}) async-start(), calls=%async_computation.7 | async-start | bytes 18874368 | tf_op jit(solution)/shard_map/all_gather | solution.py:10
  433.5 180.2 %all-gather.18.cloned.1.call-start = ((), (), s32[]{:S(2)}) async-start(), calls=%async_computation.8 | async-start | bytes 18874368 | tf_op jit(solution)/shard_map/all_gather | solution.py:10
  434.1 364.3 %reduce-scatter.5.cloned.1.call-start = ((), (), s32[]{:S(2)}) async-start(), calls=%async_computation.4 | async-start | bytes 2621440 | tf_op jit(solution)/shard_map/reduce_scatter | solution.py:72
  753.1 47.8 %copy-start.1 = (s32[4,2]{0,1:T(2,128)S(1)}, s32[4,2]{0,1:T(2,128)}, u32[]{:S(2)}) copy-start(s32[4,2]{0,1:T(2,128)} %param.18) | copy-start | bytes 100
Sparse Core Ops, SparseCore 0:
  13.2 92.4 all-gather.11
  107.6 89.7 all-gather.13
  338.4 43.6 reduce-scatter.2
  384.7 44.8 all-gather.9
  433.6 88.5 all-gather.15
  523.9 89.7 all-gather.17
  754.7 43.6 reduce-scatter.4
